TPU v7x, 256 devices: a whole 4x4x8 slice. The times are simulated.
256 devices in a mesh: pole: 4 (over y), row: 8 (over z_lo, x), col: 8 (over z_hi, core).
Axes of the slice: x: 4, y: 4, z: 8 (z_hi: 4, z_lo: 2; z = z_hi * 2 + z_lo), core: 2. Of those that a mesh axis runs over, the one named last changes fastest.
Arguments:
- found_inverse: bfloat16 [4, 2, 8192, 8, 8, 128], P('pole', None, 'row', None, 'col'), may hold values from -0.125 to 0.125
- l_panel: bfloat16 [4, 2, 8192, 512], P('pole', None, ('row', 'col')), may hold values from -1.5 to 1.5
- block_pattern: int32 [64, 4], P(('row', 'col')), may hold values 0 or 1
- sup_widths: int32 [4], replicated, may hold values from 1 to 128, 320 in all
- diag_inverse: bfloat16 [4, 2, 512, 128], P('pole'), may hold values from -6 to 6
- pole_weights: float32 [4, 2], P('pole'), may hold values from -4 to 4
Outputs:
- density: float32 [512, 8192], P('col', 'row')
- diagonal: float32 [512, 128], replicated
Inputs may be any that keep to these rules, and one draw needn't show every extreme that they name: `sup_widths`: one supernode has exactly 128 columns.
All inputs are finite; a program needn't handle non-finite values. No bound on the sum of `block_pattern` on one device may be relied on, other than what follows from the above.
Results may differ from a plain program's by a relative error of at most 0.0003.
Values may be sent and summed in bfloat16 or wider, within the bound.
A program may use at most 128 MiB of HBM per device.

v0:
```python
import jax
import jax.numpy as jnp
from jax import lax
from jax.sharding import PartitionSpec as P


def contract(left, right):
    return jnp.einsum("jk,ij->ki", left, right, preferred_element_type=jnp.float32)


def pair_product(left, right):
    return jnp.einsum("ika,kbi->kab", left, right, precision=lax.Precision.HIGHEST)


def per_device(found_inverse, l_panel, block_pattern, sup_widths, diag_inverse, pole_weights):
    slot_width = diag_inverse.shape[-1]
    total_cols = l_panel.shape[-1]
    supernodes = total_cols // slot_width
    row_count = lax.axis_size("row")
    row_index = lax.axis_index("row")
    col_index = lax.axis_index("col")
    columns = jnp.arange(total_cols, dtype=jnp.int32)
    column_ok = columns % slot_width < jnp.repeat(sup_widths, slot_width)
    block_ok = jnp.repeat(block_pattern[0], slot_width) == 1
    masked = jnp.where(
        (column_ok & block_ok)[None, None, :], l_panel[0], jnp.zeros((), jnp.bfloat16)
    )
    column_rows = lax.all_gather(masked, "row", axis=1, tiled=True)
    own_rows = lax.all_gather(masked, "col", axis=1, tiled=True)
    local_rows = found_inverse.shape[2]
    inverse = found_inverse[0].reshape(2, local_rows, row_count * slot_width)
    part_real = contract(column_rows[1], inverse[1]) - contract(column_rows[0], inverse[0])
    part_imag = -(contract(column_rows[1], inverse[0]) + contract(column_rows[0], inverse[1]))
    w_real = pole_weights[0, 0]
    w_imag = pole_weights[0, 1]
    weighted = w_real * part_real - w_imag * part_imag
    part = lax.psum_scatter(weighted, "col", scatter_dimension=0, tiled=True)
    density = lax.psum(part, "pole")
    lifted = own_rows.astype(jnp.float32).reshape(2, local_rows, supernodes, slot_width)
    upper_real = part_real.reshape(supernodes, slot_width, local_rows)
    upper_imag = part_imag.reshape(supernodes, slot_width, local_rows)
    t_real = pair_product(lifted[0], upper_real) - pair_product(lifted[1], upper_imag)
    t_imag = pair_product(lifted[0], upper_imag) + pair_product(lifted[1], upper_real)
    lead_flag = ((row_index == 0) & (col_index == 0)).astype(jnp.float32)
    d_real = diag_inverse[0, 0].astype(jnp.float32).reshape(supernodes, slot_width, slot_width)
    d_imag = diag_inverse[0, 1].astype(jnp.float32).reshape(supernodes, slot_width, slot_width)
    local_term = lead_flag * (w_real * d_real - w_imag * d_imag) - (
        w_real * t_real - w_imag * t_imag
    )
    diagonal = lax.psum(local_term.reshape(total_cols, slot_width), ("pole", "row", "col"))
    return (density, diagonal)


def solution(mesh):
    in_specs = (
        P("pole", None, "row", None, "col", None),
        P("pole", None, ("row", "col"), None),
        P(("row", "col"), None),
        P(),
        P("pole", None, None, None),
        P("pole", None),
    )
    out_specs = (P("col", "row"), P())
    return jax.shard_map(
        per_device, mesh=mesh, in_specs=in_specs, out_specs=out_specs, check_vma=False
    )
```

profile of v0, /device:TPU:2, one launch (start us, length us, event | category | flops | bytes accessed | tf_op | source)
XLA Modules:
  0.0 457.6 jit_solution(11535285280863356408)
XLA Ops:
  7.2 0.0 all-gather.3.cloned.1.call-start
  7.2 0.7 compare_bitcast_fusion
  7.9 0.7 fusion.25
  8.6 1.7 bitcast_select_fusion
  10.3 0.0 all-gather.3.cloned.1.call-update
  10.3 0.0 all-gather.5.cloned.1.call-start
  10.3 0.7 all-gather.5.cloned.1.call-update
  11.1 0.0 reduce-scatter.2.cloned.1.call-start
  11.1 1.4 fusion.28
  12.5 3.8 fusion.26
  16.3 38.6 %all-gather.3.cloned.1.call-done = bf16[2,1024,512]{2,1,0:T(8,128)(2,1)} async-done(((bf16[2,128,512]{2,1,0:T(8,128)(2,1)}), bf16[2,1024,512]{2,1,0:T(8,128)(2,1)}) %all-gather.3.cloned.1.call-update) | async-done | bytes 2097168 | tf_op jit(solution)/shard_map/all_gather | solution.py:28
  54.9 0.0 copy-start.3
  54.9 2.7 fusion.2
  57.6 0.0 copy-done.3
  57.6 0.0 copy-start.2
  57.6 1.3 fusion
  58.9 0.3 copy-done.2
  59.2 1.3 fusion.12
  60.5 4.6 %multiply_subtract_fusion = (f32[512,1024]{1,0:T(8,128)}, f32[512,1024]{1,0:T(8,128)}) fusion(f32[512,1024]{1,0:T(8,128)S(1)} %fusion.12, f32[]{:T(128)} %bitcast.7, f32[]{:T(128)} %bitcast, f32[512,1024]{1,0:T(8,128)S(1)} %fusion, bf16[128,8,8,128]{3,2,1,0:T(8,128)(2,1)S(1)} %bitcast.67, bf16[2,1024,512]{2,1,0:T(8,128)(2,1)S(1)} %copy-done.3), kind=kOutput, calls=%fused_computation.8 | convolution fusion | flops 1076363264 | bytes 11534344 | tf_op jit(solution)/shard_map/jk,ij->ki/dot_general | solution.py:8
  65.1 0.0 copy-start.4
  65.1 0.0 reduce-scatter.2.cloned.1.call-update
  65.1 0.0 all-reduce.5.cloned.1.call-start
  65.2 0.9 copy-done.4
  66.1 1.3 subtract_multiply_fusion
  67.4 27.9 %all-gather.5.cloned.1.call-done = bf16[2,1024,512]{2,1,0:T(8,128)(2,1)} async-done(((bf16[2,128,512]{2,1,0:T(8,128)(2,1)}), bf16[2,1024,512]{2,1,0:T(8,128)(2,1)}) %all-gather.5.cloned.1.call-update) | async-done | bytes 2097168 | tf_op jit(solution)/shard_map/all_gather | solution.py:29
  95.3 2.7 fusion.27
  97.9 1.3 copy.8
  99.3 1.5 copy.9
  100.8 0.0 copy-start
  100.8 0.0 copy-start.1
  100.8 2.5 fusion.29
  103.3 0.0 copy-done
  103.3 0.0 copy-done.1
  103.3 1.2 fusion.30
  104.5 1.9 fusion.20
  106.4 2.5 fusion.19
  108.9 0.0 all-reduce.5.cloned.1.call-update
  108.9 0.0 all-reduce.3.cloned.1.call-start
  109.0 31.0 %reduce-scatter.2.cloned.1.call-done = f32[64,1024]{1,0:T(8,128)} async-done(((f32[512,1024]{1,0:T(8,128)}), f32[64,1024]{1,0:T(8,128)}) %reduce-scatter.2.cloned.1.call-update) | async-done | bytes 262160 | tf_op jit(solution)/shard_map/reduce_scatter | solution.py:37
  140.0 0.0 all-reduce.3.cloned.1.call-update
  140.1 259.7 %all-reduce.5.cloned.1.call-done = f32[512,128]{1,0:T(8,128)} async-done(((f32[512,128]{1,0:T(8,128)}), f32[512,128]{1,0:T(8,128)}) %all-reduce.5.cloned.1.call-update) | async-done | bytes 262160 | tf_op jit(solution)/shard_map/psum | solution.py:50
  399.8 48.0 %all-reduce.3.cloned.1.call-done = f32[64,1024]{1,0:T(8,128)} async-done(((f32[64,1024]{1,0:T(8,128)}), f32[64,1024]{1,0:T(8,128)}) %all-reduce.3.cloned.1.call-update) | async-done | bytes 262160 | tf_op jit(solution)/shard_map/psum | solution.py:38
  447.8 1.7 copy.36
  449.4 1.7 copy.37
Async XLA Ops:
  7.2 47.7 %all-gather.3.cloned.1.call-start = ((), (), s32[]{:S(2)}) async-start(), calls=%async_computation.1 | async-start | bytes 2359296 | tf_op jit(solution)/shard_map/all_gather | solution.py:28
  10.3 85.0 %all-gather.5.cloned.1.call-start = ((), (), s32[]{:S(2)}) async-start(), calls=%async_computation.4 | async-start | bytes 2359296 | tf_op jit(solution)/shard_map/all_gather | solution.py:29
  11.1 129.0 %reduce-scatter.2.cloned.1.call-start = ((), (), s32[]{:S(2)}) async-start(), calls=%async_computation.2 | async-start | bytes 2359296 | tf_op jit(solution)/shard_map/reduce_scatter | solution.py:37
  54.9 2.7 copy-start.3
  57.6 1.6 copy-start.2
  65.1 0.9 copy-start.4
  65.1 334.7 %all-reduce.5.cloned.1.call-start = ((), (), s32[]{:S(2)}) async-start(), calls=%async_computation.5 | async-start | bytes 524288 | tf_op jit(solution)/shard_map/psum | solution.py:50
  100.8 2.6 copy-start
  100.8 2.6 copy-start.1
  108.9 338.8 %all-reduce.3.cloned.1.call-start = ((), (), s32[]{:S(2)}) async-start(), calls=%async_computation.3 | async-start | bytes 524288 | tf_op jit(solution)/shard_map/psum | solution.py:38
Sparse Core Ops, SparseCore 0:
  10.4 44.4 all-gather.2
  57.3 37.9 all-gather.4
  97.8 42.1 reduce-scatter.1
  145.9 253.8 all-reduce.4
  402.0 45.7 all-reduce.2
where the time goes:
time: 458 us
  waiting for transfers between devices  406 us (89%)
  matrix products  18 us (4%)
  local copies, waits for them, and re-layouts  15.2 us (3%)
  between operations  13.9 us (3%)
    psum x1, waiting for transfers between devices, per_device(): lax.psum(local_term.reshape(total_cols, slot_width), ('pole', 'row', 'col'))  260 us
    psum x1, waiting for transfers between devices, per_device(): density = lax.psum(part, 'pole')  48 us
    all_gather x1, waiting for transfers between devices, per_device(): column_rows = lax.all_gather(masked, 'row', axis=1, tiled=True)  38.6 us
    reduce_scatter x1, waiting for transfers between devices, per_device(): part = lax.psum_scatter(weighted, 'col', scatter_dimension=0, tiled=True)  31 us
    all_gather x1, waiting for transfers between devices, per_device(): own_rows = lax.all_gather(masked, 'col', axis=1, tiled=True)  27.9 us
    dot_general x4, matrix products, contract(): jnp.einsum('jk,ij->ki', left, right, preferred_element_type=jnp.float32)  9.92 us
  transfers between devices with their start and end apart: 5, of which 5 were waited for; matrix products, arithmetic and copies ran while one was open for 7% of the time, Pallas kernels for 0%

commit v1 on v0

--- a/solution.py
+++ b/solution.py
@@ -25,7 +25,9 @@
     masked = jnp.where(
         (column_ok & block_ok)[None, None, :], l_panel[0], jnp.zeros((), jnp.bfloat16)
     )
-    column_rows = lax.all_gather(masked, "row", axis=1, tiled=True)
+    column_rows = jnp.concatenate(
+        lax.all_to_all(jnp.stack([masked] * lax.axis_size("row")), "row", 0, 0), axis=1
+    )
     own_rows = lax.all_gather(masked, "col", axis=1, tiled=True)
     local_rows = found_inverse.shape[2]
     inverse = found_inverse[0].reshape(2, local_rows, row_count * slot_width)

time: 458 us -> 433 us (0.945)
  waiting for transfers between devices: 406 us -> 373 us
  starting transfers between devices: 0.2 us -> 6.62 us
    all_gather x1 -> x0, waiting for transfers between devices: 38.6 us -> none  [per_device(): column_rows = lax.all_gather(masked, 'row', axis=1, tiled=True)]
    all_to_all x0 -> x1, waiting for transfers between devices: none -> 30.2 us  [per_device(): lax.all_to_all(jnp.stack([masked] * lax.axis_size('row')), 'row', 0, 0)]
    all_gather x1, waiting for transfers between devices: 27.9 us -> 0.02 us  [per_device(): own_rows = lax.all_gather(masked, 'col', axis=1, tiled=True)]
    all_to_all x0 -> x1, starting transfers between devices: none -> 6.32 us  [per_device(): lax.all_to_all(jnp.stack([masked] * lax.axis_size('row')), 'row', 0, 0)]
  transfers between devices with their start and end apart: 5 -> 5, of which waited for: 5 -> 4; matrix products, arithmetic and copies ran while one was open for 7% -> 7% of each run, Pallas kernels for 0% -> 0%
where the time goes in v1:
time: 433 us; the launch traced here: 432 us
  waiting for transfers between devices  373 us (86%)
  local copies, waits for them, and re-layouts  18 us (4%)
  matrix products  16.7 us (4%)
  between operations  13.9 us (3%)
  starting transfers between devices  6.62 us (2%)
  other arithmetic  4.4 us (1%)
    psum x1, waiting for transfers between devices, per_device(): lax.psum(local_term.reshape(total_cols, slot_width), ('pole', 'row', 'col'))  260 us
    psum x1, waiting for transfers between devices, per_device(): density = lax.psum(part, 'pole')  48 us
    reduce_scatter x1, waiting for transfers between devices, per_device(): part = lax.psum_scatter(weighted, 'col', scatter_dimension=0, tiled=True)  34.4 us
    all_to_all x1, waiting for transfers between devices, per_device(): lax.all_to_all(jnp.stack([masked] * lax.axis_size('row')), 'row', 0, 0)  30.2 us
  transfers between devices with their start and end apart: 5, of which 4 were waited for; matrix products, arithmetic and copies ran while one was open for 7% of the time, Pallas kernels for 0%

profile of v1, /device:TPU:2, one launch (start us, length us, event | category | flops | bytes accessed | tf_op | source)
XLA Modules:
  0.0 432.3 jit_solution(3155090668460693979)
XLA Ops:
  7.2 0.7 compare_bitcast_fusion
  7.8 0.7 fusion.25
  8.6 1.0 select_bitcast_fusion
  9.5 1.5 stack.5
  11.1 0.0 copy-start.4
  11.1 0.0 copy-start.6
  11.1 6.3 %all-to-all-start = ((bf16[8,2,128,512]{3,2,1,0:T(8,128)(2,1)}), bf16[8,2,128,512]{3,2,1,0:T(8,128)(2,1)S(1)}, u32[]{:S(2)}, u32[]{:S(2)}) async-start(bf16[8,2,128,512]{3,2,1,0:T(8,128)(2,1)} %stack.5), calls=%async_computation | async-start | bytes 4194304 | tf_op jit(solution)/shard_map/all_to_all | solution.py:29
  17.4 0.0 all-gather.2.cloned.1.call-start
  17.4 0.0 copy-done.4
  17.4 0.7 bitcast_select_fusion
  18.1 0.0 all-gather.2.cloned.1.call-update
  18.1 0.0 reduce-scatter.2.cloned.1.call-start
  18.2 0.0 copy-done.6
  18.2 0.6 fusion.29
  18.8 4.5 %fusion.26 = (bf16[1,1,1024,8,1,128]{5,3,4,2,1,0:T(8,128)(2,1)}, bf16[1,1,1024,8,1,128]{5,3,4,2,1,0:T(8,128)(2,1)}) fusion(bf16[1,2,1024,8,1,128]{5,3,4,2,1,0:T(8,128)(2,1)} %param.6), kind=kLoop, calls=%fused_computation.32 | loop fusion | bytes 8388608 | tf_op jit(solution)/shard_map/slice | solution.py:34
  23.3 30.2 %all-to-all-done = bf16[8,2,128,512]{3,2,1,0:T(8,128)(2,1)S(1)} async-done(((bf16[8,2,128,512]{3,2,1,0:T(8,128)(2,1)}), bf16[8,2,128,512]{3,2,1,0:T(8,128)(2,1)S(1)}, u32[]{:S(2)}, u32[]{:S(2)}) %all-to-all-start) | async-done | bytes 2097184 | tf_op jit(solution)/shard_map/all_to_all | solution.py:29
  53.4 0.0 copy-start.3
  53.4 0.2 fusion.28
  53.6 1.4 copy-done.3
  55.0 1.3 fusion.2
  56.3 0.0 copy-start.2
  56.3 1.3 fusion
  57.6 0.3 copy-done.2
  58.0 1.3 fusion.12
  59.3 4.7 %multiply_subtract_fusion = (f32[512,1024]{1,0:T(8,128)}, f32[512,1024]{1,0:T(8,128)}) fusion(f32[512,1024]{1,0:T(8,128)S(1)} %fusion.12, f32[]{:T(128)} %bitcast.8, f32[]{:T(128)} %bitcast, f32[512,1024]{1,0:T(8,128)S(1)} %fusion, bf16[1024,512]{1,0:T(8,128)(2,1)S(1)} %bitcast.69, bf16[128,8,8,128]{3,2,1,0:T(8,128)(2,1)S(1)} %bitcast.67), kind=kOutput, calls=%fused_computation.8 | convolution fusion | flops 1076363264 | bytes 11534344 | tf_op jit(solution)/shard_map/jk,ij->ki/dot_general | solution.py:8
  64.0 0.0 copy-start.5
  64.0 0.0 reduce-scatter.2.cloned.1.call-update
  64.0 0.2 all-reduce.5.cloned.1.call-start
  64.2 0.7 copy-done.5
  64.9 1.3 subtract_multiply_fusion
  66.3 0.0 all-gather.2.cloned.1.call-done
  66.3 2.7 fusion.27
  69.0 1.3 copy.8
  70.3 1.5 copy.9
  71.8 0.0 copy-start
  71.8 0.0 copy-start.1
  71.8 2.5 fusion.30
  74.3 0.0 copy-done
  74.3 0.0 copy-done.1
  74.4 1.2 fusion.31
  75.5 1.9 fusion.20
  77.4 2.5 fusion.19
  79.9 0.0 all-reduce.5.cloned.1.call-update
  80.0 0.0 all-reduce.3.cloned.1.call-start
  80.0 34.4 %reduce-scatter.2.cloned.1.call-done = f32[64,1024]{1,0:T(8,128)} async-done(((f32[512,1024]{1,0:T(8,128)}), f32[64,1024]{1,0:T(8,128)}) %reduce-scatter.2.cloned.1.call-update) | async-done | bytes 262160 | tf_op jit(solution)/shard_map/reduce_scatter | solution.py:39
  114.4 0.0 all-reduce.3.cloned.1.call-update
  114.5 259.9 %all-reduce.5.cloned.1.call-done = f32[512,128]{1,0:T(8,128)} async-done(((f32[512,128]{1,0:T(8,128)}), f32[512,128]{1,0:T(8,128)}) %all-reduce.5.cloned.1.call-update) | async-done | bytes 262160 | tf_op jit(solution)/shard_map/psum | solution.py:52
  374.4 48.0 %all-reduce.3.cloned.1.call-done = f32[64,1024]{1,0:T(8,128)} async-done(((f32[64,1024]{1,0:T(8,128)}), f32[64,1024]{1,0:T(8,128)}) %all-reduce.3.cloned.1.call-update) | async-done | bytes 262160 | tf_op jit(solution)/shard_map/psum | solution.py:40
  422.4 1.7 copy.36
  424.1 1.7 copy.37
Async XLA Ops:
  11.1 6.3 %copy-start.4 = (bf16[1,2,128,512]{3,2,1,0:T(8,128)(2,1)S(1)}, bf16[1,2,128,512]{3,2,1,0:T(8,128)(2,1)}, u32[]{:S(2)}) copy-start(bf16[1,2,128,512]{3,2,1,0:T(8,128)(2,1)} %param.7) | copy-start | bytes 786436
  11.1 7.1 %copy-start.6 = (f32[1,2]{1,0:T(1,128)S(1)}, f32[1,2]{1,0:T(1,128)}, u32[]{:S(2)}) copy-start(f32[1,2]{1,0:T(1,128)} %param.11) | copy-start | bytes 28
  11.1 42.4 %all-to-all-start = ((bf16[8,2,128,512]{3,2,1,0:T(8,128)(2,1)}), bf16[8,2,128,512]{3,2,1,0:T(8,128)(2,1)S(1)}, u32[]{:S(2)}, u32[]{:S(2)}) async-start(bf16[8,2,128,512]{3,2,1,0:T(8,128)(2,1)} %stack.5), calls=%async_computation | async-start | bytes 4194304 | tf_op jit(solution)/shard_map/all_to_all | solution.py:29
  17.4 48.9 %all-gather.2.cloned.1.call-start = ((), (), s32[]{:S(2)}) async-start(), calls=%async_computation.4 | async-start | bytes 2359296 | tf_op jit(solution)/shard_map/all_gather | solution.py:31
  18.1 96.3 %reduce-scatter.2.cloned.1.call-start = ((), (), s32[]{:S(2)}) async-start(), calls=%async_computation.2 | async-start | bytes 2359296 | tf_op jit(solution)/shard_map/reduce_scatter | solution.py:39
  53.4 1.6 copy-start.3
  56.3 1.6 copy-start.2
  64.0 0.9 copy-start.5
  64.0 310.4 %all-reduce.5.cloned.1.call-start = ((), (), s32[]{:S(2)}) async-start(), calls=%async_computation.5 | async-start | bytes 524288 | tf_op jit(solution)/shard_map/psum | solution.py:52
  71.8 2.6 copy-start
  71.8 2.6 copy-start.1
  80.0 342.5 %all-reduce.3.cloned.1.call-start = ((), (), s32[]{:S(2)}) async-start(), calls=%async_computation.3 | async-start | bytes 524288 | tf_op jit(solution)/shard_map/psum | solution.py:40
Sparse Core Ops, SparseCore 0:
  20.6 43.3 all-gather.1
  66.6 47.8 reduce-scatter.1
  120.5 253.8 all-reduce.4
  376.6 45.7 all-reduce.2
